TPU v7x, 256 devices: a whole 4x4x8 slice. The times are simulated.
256 devices in a mesh: seq: 8 (over z), expert: 8 (over y, core), mp: 4 (over x).
Axes of the slice: x: 4, y: 4, z: 8, core: 2. Of those that a mesh axis runs over, the one named last changes fastest.
Arguments:
- tokens: bfloat16 [2048, 6144], P(('seq', 'expert', 'mp')), may hold values from -6 to 6
- out_grad: bfloat16 [2048, 6144], P(('seq', 'expert', 'mp')), may hold values from -3 to 3
- kept_mask: int32 [2048], P(('seq', 'expert', 'mp')), may hold values 0 or 1
- routes: int32 [2048, 2], P(('seq', 'expert', 'mp')), may hold values from 0 to 7, all different within a row; in each aligned block of 8 rows (0 to 7, 8 to 15, ...) at most 3 rows name the same one
- router: bfloat16 [6144, 8], replicated, may hold values from -0.078125 to 0.078125
- gate_weight: bfloat16 [8, 6144, 8192], P('expert', None, ('seq', 'mp')), may hold values from -0.078125 to 0.078125
- up_weight: bfloat16 [8, 6144, 8192], P('expert', None, ('seq', 'mp')), may hold values from -0.078125 to 0.078125
- down_weight: bfloat16 [8, 8192, 6144], P('expert', ('seq', 'mp')), may hold values from -0.0625 to 0.0625
Outputs:
- d_tokens: bfloat16 [2048, 6144], P(('seq', 'expert', 'mp'))
- gate_grad: float32 [2048, 2], P(('seq', 'expert', 'mp'))
Inputs may be any that keep to these rules, and one draw needn't show every extreme that they name: `routes`: among the 8 rows of one device, at most 3 name any one expert, and in every draw some expert is named by exactly 3 rows of some device.
All inputs are finite; a program needn't handle non-finite values. No bound on the sum of `kept_mask` on one device may be relied on, other than what follows from the above.
Results may differ from a plain program's by a relative error of at most 0.02.
Values may be sent and summed in bfloat16 or wider, within the bound.
A program may use at most 128 MiB of HBM per device.

v0:
```python
import jax
import jax.numpy as jnp
from jax import lax
from jax.sharding import PartitionSpec as P


def on_device(tokens, out_grad, kept_mask, routes, router, gate_weight, up_weight, down_weight):
    row_count = tokens.shape[0]
    width = tokens.shape[1]
    expert_count = lax.axis_size("expert")
    capacity = max(3 * row_count // 8, 2 * row_count // expert_count)
    logits = jnp.dot(tokens, router, preferred_element_type=jnp.float32)
    columns = lax.broadcasted_iota(jnp.int32, (row_count, expert_count), 1)
    first_hot = (routes[:, 0:1] == columns).astype(jnp.float32)
    second_hot = (routes[:, 1:2] == columns).astype(jnp.float32)
    first_logit = jnp.sum(logits * first_hot, axis=1)
    second_logit = jnp.sum(logits * second_hot, axis=1)
    gate_first = jax.nn.sigmoid(first_logit - second_logit)
    gate_second = jax.nn.sigmoid(second_logit - first_logit)
    keep_rows = kept_mask.astype(jnp.float32)
    chosen = ((first_hot + second_hot) * keep_rows[:, None]).astype(jnp.int32)
    position = jnp.cumsum(chosen, axis=0) - 1
    slot_iota = lax.broadcasted_iota(jnp.int32, (row_count, expert_count, capacity), 2)
    select_mask = (chosen[:, :, None] == 1) & (position[:, :, None] == slot_iota)
    select_bf = select_mask.astype(jnp.bfloat16)
    select_full = select_mask.astype(jnp.float32)
    token_send = jnp.einsum(
        "tec,td->ecd", select_bf, tokens, preferred_element_type=jnp.float32
    ).astype(jnp.bfloat16)
    grad_send = jnp.einsum(
        "tec,td->ecd", select_bf, out_grad, preferred_element_type=jnp.float32
    ).astype(jnp.bfloat16)
    gate_table = first_hot * gate_first[:, None] + second_hot * gate_second[:, None]
    gate_send = jnp.einsum(
        "tec,te->ec", select_full, gate_table, precision=lax.Precision.HIGHEST
    ).astype(jnp.bfloat16)
    token_recv, grad_recv, gate_recv = (
        lax.all_to_all(token_send, "expert", split_axis=0, concat_axis=0, tiled=True),
        lax.all_to_all(grad_send, "expert", split_axis=0, concat_axis=0, tiled=True),
        lax.all_to_all(gate_send, "expert", split_axis=0, concat_axis=0, tiled=True),
    )
    token_all, grad_all, gate_all = (
        lax.all_gather(token_recv, ("seq", "mp"), axis=0, tiled=True),
        lax.all_gather(grad_recv, ("seq", "mp"), axis=0, tiled=True),
        lax.all_gather(gate_recv, ("seq", "mp"), axis=0, tiled=True),
    )
    token_all = token_all.reshape(-1, width)
    grad_all = grad_all.reshape(-1, width)
    gate_all = gate_all.reshape(-1)
    gate_local = gate_weight[0]
    up_local = up_weight[0]
    down_local = down_weight[0]
    pre_gate = jnp.dot(token_all, gate_local, preferred_element_type=jnp.float32)
    pre_up = jnp.dot(token_all, up_local, preferred_element_type=jnp.float32)
    sigma = jax.nn.sigmoid(pre_gate)
    act = pre_gate * sigma
    hidden = act * pre_up
    grad_hidden = jnp.dot(grad_all, down_local.T, preferred_element_type=jnp.float32)
    gate_dot = jnp.sum(grad_hidden * hidden, axis=1)
    scaled = gate_all.astype(jnp.float32)[:, None] * grad_hidden
    grad_gate = (scaled * pre_up * sigma * (1.0 + pre_gate * (1.0 - sigma))).astype(jnp.bfloat16)
    grad_up = (scaled * act).astype(jnp.bfloat16)
    expert_grad = jnp.dot(grad_gate, gate_local.T, preferred_element_type=jnp.float32)
    expert_grad = expert_grad + jnp.dot(grad_up, up_local.T, preferred_element_type=jnp.float32)
    grad_own = lax.psum_scatter(
        expert_grad.astype(jnp.bfloat16), ("seq", "mp"), scatter_dimension=0, tiled=True
    ).astype(jnp.float32)
    dot_own = lax.psum_scatter(gate_dot, ("seq", "mp"), scatter_dimension=0, tiled=True)
    grad_back, dot_back = (
        lax.all_to_all(
            grad_own.reshape(expert_count, capacity, width).astype(jnp.bfloat16),
            "expert",
            split_axis=0,
            concat_axis=0,
            tiled=True,
        ).astype(jnp.float32),
        lax.all_to_all(
            dot_own.reshape(expert_count, capacity).astype(jnp.bfloat16),
            "expert",
            split_axis=0,
            concat_axis=0,
            tiled=True,
        ).astype(jnp.float32),
    )
    expert_sum = jnp.einsum("tec,ecd->td", select_full, grad_back, precision=lax.Precision.HIGHEST)
    dot_table = jnp.einsum("tec,ec->te", select_full, dot_back, precision=lax.Precision.HIGHEST)
    dot_first = jnp.sum(dot_table * first_hot, axis=1)
    dot_second = jnp.sum(dot_table * second_hot, axis=1)
    product = gate_first * gate_second * keep_rows
    grad_first = product * (dot_first - dot_second)
    grad_second = product * (dot_second - dot_first)
    logit_grad = first_hot * grad_first[:, None] + second_hot * grad_second[:, None]
    router_term = jnp.dot(logit_grad, router.astype(jnp.float32).T, precision=lax.Precision.HIGHEST)
    d_tokens = ((expert_sum + router_term) * keep_rows[:, None]).astype(jnp.bfloat16)
    gate_grad = jnp.stack([grad_first, grad_second], axis=1)
    return (d_tokens, gate_grad)


def solution(mesh):
    return jax.shard_map(
        on_device,
        mesh=mesh,
        in_specs=(
            P(("seq", "expert", "mp"), None),
            P(("seq", "expert", "mp"), None),
            P(("seq", "expert", "mp")),
            P(("seq", "expert", "mp"), None),
            P(),
            P("expert", None, ("seq", "mp")),
            P("expert", None, ("seq", "mp")),
            P("expert", ("seq", "mp"), None),
        ),
        out_specs=(P(("seq", "expert", "mp"), None), P(("seq", "expert", "mp"), None)),
        check_vma=False,
    )
```

profile of v0, /device:TPU:1, one launch (start us, length us, event | category | flops | bytes accessed | tf_op | source)
XLA Modules:
  0.0 688.7 jit_solution(3209703216275535613)
XLA Ops:
  11.1 13.9 %all_to_all.36 = bf16[8,3,6144]{2,1,0:T(4,128)(2,1)S(1)} all-to-all(bf16[8,3,6144]{2,1,0:T(4,128)(2,1)S(1)} %copy.43), channel_id=1, replica_groups=mesh['seq'=8,'expert'=8,'mp'=4] {'expert'}, dimensions={0} | all-to-all | bytes 589824 | tf_op jit(solution)/shard_map/all_to_all | solution.py:38
  27.4 11.3 %all_to_all.37 = bf16[8,3,6144]{2,1,0:T(4,128)(2,1)S(1)} all-to-all(bf16[8,3,6144]{2,1,0:T(4,128)(2,1)S(1)} %copy.39), channel_id=1, replica_groups=mesh['seq'=8,'expert'=8,'mp'=4] {'expert'}, dimensions={0} | all-to-all | bytes 589824 | tf_op jit(solution)/shard_map/all_to_all | solution.py:39
  39.7 1.3 dynamic-slice
  41.7 88.6 %all-gather.6.cloned.1.call-done = bf16[256,3,6144]{2,0,1:T(8,128)(2,1)} async-done(((bf16[8,3,6144]{2,0,1:T(8,128)(2,1)}), bf16[256,3,6144]{2,0,1:T(8,128)(2,1)}) %all-gather.6.cloned.1.call-update) | async-done | bytes 9437200 | tf_op jit(solution)/shard_map/all_gather | solution.py:43
  130.3 14.7 %copy.45 = bf16[256,3,6144]{2,1,0:T(4,128)(2,1)} copy(bf16[256,3,6144]{2,0,1:T(8,128)(2,1)} %all-gather.6.cloned.1.call-done) | data formatting | bytes 18874368 | tf_op jit(solution)/shard_map/all_gather | solution.py:43
  145.0 23.6 %reshape.179 = bf16[768,6144]{1,0:T(8,128)(2,1)} reshape(bf16[256,3,6144]{2,1,0:T(4,128)(2,1)} %copy.45) | data formatting | bytes 18874368 | tf_op jit(solution)/shard_map/reshape | solution.py:47
  168.5 7.4 %fusion.4 = f32[768,256]{0,1:T(8,128)} fusion(bf16[768,6144]{1,0:T(8,128)(2,1)} %reshape.179, bf16[1,6144,256]{2,1,0:T(8,128)(2,1)S(1)} %copy-done), kind=kOutput, calls=%fused_computation.9 | convolution fusion | flops 2415919104 | bytes 13369344 | tf_op jit(solution)/shard_map/dot_general | solution.py:53
  175.9 3.8 fusion.7
  179.7 53.8 %all-gather.4.cloned.1.call-done = bf16[256,3,6144]{2,0,1:T(8,128)(2,1)} async-done(((bf16[8,3,6144]{2,0,1:T(8,128)(2,1)}), bf16[256,3,6144]{2,0,1:T(8,128)(2,1)}) %all-gather.4.cloned.1.call-update) | async-done | bytes 9437200 | tf_op jit(solution)/shard_map/all_gather | solution.py:44
  233.5 14.7 %copy.41 = bf16[256,3,6144]{2,1,0:T(4,128)(2,1)} copy(bf16[256,3,6144]{2,0,1:T(8,128)(2,1)} %all-gather.4.cloned.1.call-done) | data formatting | bytes 18874368 | tf_op jit(solution)/shard_map/all_gather | solution.py:44
  248.2 23.5 %reshape.178 = bf16[768,6144]{1,0:T(8,128)(2,1)} reshape(bf16[256,3,6144]{2,1,0:T(4,128)(2,1)} %copy.41) | data formatting | bytes 18874368 | tf_op jit(solution)/shard_map/reshape | solution.py:48
  271.7 8.6 %multiply_reduce_fusion = (f32[768]{0:T(1024)S(1)}, f32[768,256]{0,1:T(8,128)}) fusion(f32[768,256]{0,1:T(8,128)} %fusion.7, f32[768,256]{0,1:T(8,128)} %fusion.4, bf16[768,6144]{1,0:T(8,128)(2,1)} %reshape.178, bf16[1,256,6144]{2,1,0:T(8,128)(2,1)} %param.15), kind=kOutput, calls=%fused_computation.16 | convolution fusion | flops 2417294592 | bytes 14945280 | tf_op jit(solution)/shard_map/dot_general | solution.py:58
  280.3 57.6 %all-reduce = bf16[768]{0:T(1024)(128)(2,1)S(1)} all-reduce(f32[768]{0:T(1024)S(1)} %get-tuple-element.13), channel_id=4, replica_groups=mesh['seq'=8,'expert'=8,'mp'=4] {'seq','mp'}, use_global_device_ids=true, to_apply=%region_5.6.clone | all-reduce | flops 768 | bytes 4608
  338.0 23.4 %all_to_all.38 = bf16[8,1,3]{2,1,0:T(2,128)(2,1)S(1)} all-to-all(bf16[8,1,3]{2,1,0:T(2,128)(2,1)S(1)} %convert_element_type.108), channel_id=1, replica_groups=mesh['seq'=8,'expert'=8,'mp'=4] {'expert'}, dimensions={0} | all-to-all | bytes 96 | tf_op jit(solution)/shard_map/all_to_all | solution.py:77
  362.6 7.6 %all_to_all.39 = bf16[8,1,3]{2,1,0:T(2,128)(2,1)S(1)} all-to-all(bf16[8,1,3]{2,1,0:T(2,128)(2,1)S(1)} %copy.37), channel_id=1, replica_groups=mesh['seq'=8,'expert'=8,'mp'=4] {'expert'}, dimensions={0} | all-to-all | bytes 96 | tf_op jit(solution)/shard_map/all_to_all | solution.py:40
  370.2 30.7 %all-gather = bf16[256,1,3]{2,1,0:T(2,128)(2,1)S(1)} all-gather(bf16[8,1,3]{2,1,0:T(2,128)(2,1)S(1)} %all_to_all.39), channel_id=2, replica_groups=mesh['seq'=8,'expert'=8,'mp'=4] {'seq','mp'}, dimensions={0}, use_global_device_ids=true | all-gather | bytes 1584 | tf_op jit(solution)/shard_map/all_gather | solution.py:45
  401.5 9.7 %fusion.2 = f32[768,6144]{1,0:T(8,128)} fusion(bf16[1,6144,256]{2,1,0:T(8,128)(2,1)S(1)} %copy-done, f32[768,256]{0,1:T(8,128)} %fusion.4, f32[768,256]{0,1:T(8,128)} %fusion.7, f32[768,256]{0,1:T(8,128)} %get-tuple-element.14, f32[768]{0:T(1024)S(1)} %reshape.180), kind=kOutput, calls=%fused_computation.7 | convolution fusion | flops 2418081792 | bytes 24382464 | tf_op jit(solution)/shard_map/dot_general | solution.py:63
  411.2 14.2 %add_convert_fusion = bf16[768,6144]{1,0:T(8,128)(2,1)} fusion(f32[768,6144]{1,0:T(8,128)} %fusion.2, bf16[1,6144,256]{2,1,0:T(8,128)(2,1)} %param.14, f32[768,256]{0,1:T(8,128)} %get-tuple-element.14, f32[768]{0:T(1024)S(1)} %reshape.180, f32[768,256]{0,1:T(8,128)} %fusion.4), kind=kOutput, calls=%fused_computation | convolution fusion | flops 2426732544 | bytes 33033216 | tf_op jit(solution)/shard_map/dot_general | solution.py:64
  425.5 235.6 %reduce-scatter.2.cloned.1.call-done = bf16[24,6144]{1,0:T(8,128)(2,1)} async-done(((bf16[768,6144]{1,0:T(8,128)(2,1)}), bf16[24,6144]{1,0:T(8,128)(2,1)}) %reduce-scatter.2.cloned.1.call-update) | async-done | bytes 294928 | tf_op jit(solution)/shard_map/reduce_scatter | solution.py:65
  661.1 1.9 convert_element_type.102
  662.9 9.0 %all-to-all-start.3 = ((bf16[8,3,6144]{2,1,0:T(4,128)(2,1)}), bf16[8,3,6144]{2,1,0:T(4,128)(2,1)S(1)}, u32[]{:S(2)}, u32[]{:S(2)}) async-start(bf16[8,3,6144]{2,1,0:T(4,128)(2,1)} %convert_element_type.102), calls=%async_computation.4 | async-start | bytes 786432 | tf_op jit(solution)/shard_map/all_to_all | solution.py:70
  673.2 1.2 pad_maximum_fusion
  674.3 5.7 all-to-all-done.3
  680.3 1.8 fusion.1
  (60 shorter events, 10.8 us)
Async XLA Ops:
  7.2 161.4 %copy-start = (bf16[1,6144,256]{2,1,0:T(8,128)(2,1)S(1)}, bf16[1,6144,256]{2,1,0:T(8,128)(2,1)}, u32[]{:S(2)}) copy-start(bf16[1,6144,256]{2,1,0:T(8,128)(2,1)} %param.13) | copy-start | bytes 9437188
  7.2 123.1 %all-gather.6.cloned.1.call-start = ((), (), s32[]{:S(2)}) async-start(), calls=%async_computation.7 | async-start | bytes 9732096 | tf_op jit(solution)/shard_map/all_gather | solution.py:43
  8.8 0.5 copy-start.5
  25.9 207.6 %all-gather.4.cloned.1.call-start = ((), (), s32[]{:S(2)}) async-start(), calls=%async_computation.6 | async-start | bytes 9732096 | tf_op jit(solution)/shard_map/all_gather | solution.py:44
  39.7 621.4 %reduce-scatter.2.cloned.1.call-start = ((), (), s32[]{:S(2)}) async-start(), calls=%async_computation.8 | async-start | bytes 9732096 | tf_op jit(solution)/shard_map/reduce_scatter | solution.py:65
  168.5 7.4 %copy-start.1 = (bf16[768,6144]{1,0:T(8,128)(2,1)S(1)}, bf16[768,6144]{1,0:T(8,128)(2,1)}, u32[]{:S(2)}) copy-start(bf16[768,6144]{1,0:T(8,128)(2,1)} %reshape.179) | copy-start | bytes 28311556
  168.5 7.4 %copy-start.2 = (bf16[1,6144,256]{2,1,0:T(8,128)(2,1)S(1)}, bf16[1,6144,256]{2,1,0:T(8,128)(2,1)}, u32[]{:S(2)}) copy-start(bf16[1,6144,256]{2,1,0:T(8,128)(2,1)} %param.14) | copy-start | bytes 9437188
  271.7 89.9 %copy-start.3 = (bf16[8,6144]{1,0:T(8,128)(2,1)S(1)}, bf16[8,6144]{1,0:T(8,128)(2,1)}, u32[]{:S(2)}) copy-start(bf16[8,6144]{1,0:T(8,128)(2,1)} %param.8) | copy-start | bytes 294916
  271.7 89.9 %copy-start.4 = (bf16[6144,8]{0,1:T(8,128)(2,1)S(1)}, bf16[6144,8]{0,1:T(8,128)(2,1)}, u32[]{:S(2)}) copy-start(bf16[6144,8]{0,1:T(8,128)(2,1)} %param.12) | copy-start | bytes 294916
  271.7 90.1 %copy-start.11 = (s32[8]{0:T(128)S(1)}, s32[8]{0:T(128)}, u32[]{:S(2)}) copy-start(s32[8]{0:T(128)} %param.10) | copy-start | bytes 100
  361.8 49.4 %copy-start.7 = (f32[8]{0:T(128)}, f32[8]{0:T(128)S(1)}, u32[]{:S(2)}) copy-start(f32[8]{0:T(128)S(1)} %get-tuple-element.6) | copy-start | bytes 100
  361.8 49.3 %copy-start.8 = (f32[8]{0:T(128)}, f32[8]{0:T(128)S(1)}, u32[]{:S(2)}) copy-start(f32[8]{0:T(128)S(1)} %get-tuple-element.7) | copy-start | bytes 100
  362.4 48.8 %copy-start.9 = (f32[8]{0:T(128)}, f32[8]{0:T(128)S(1)}, u32[]{:S(2)}) copy-start(f32[8]{0:T(128)S(1)} %get-tuple-element.9) | copy-start | bytes 100
  362.4 48.8 %copy-start.10 = (f32[8]{0:T(128)}, f32[8]{0:T(128)S(1)}, u32[]{:S(2)}) copy-start(f32[8]{0:T(128)S(1)} %get-tuple-element.10) | copy-start | bytes 100
  662.9 17.0 %all-to-all-start.3 = ((bf16[8,3,6144]{2,1,0:T(4,128)(2,1)}), bf16[8,3,6144]{2,1,0:T(4,128)(2,1)S(1)}, u32[]{:S(2)}, u32[]{:S(2)}) async-start(bf16[8,3,6144]{2,1,0:T(4,128)(2,1)} %convert_element_type.102), calls=%async_computation.4 | async-start | bytes 786432 | tf_op jit(solution)/shard_map/all_to_all | solution.py:70
  672.6 0.5 copy-start.6
Sparse Core Ops, SparseCore 0:
  26.0 104.1 all-gather.5
  132.9 100.5 all-gather.3
  425.6 235.4 reduce-scatter.1
where the time goes:
time: 690 us; the launch traced here: 689 us
  waiting for transfers between devices  384 us (56%)
  blocking collectives  144 us (21%)
  local copies, waits for them, and re-layouts  84.8 us (12%)
  matrix products  48.3 us (7%)
  between operations  14.5 us (2%)
  starting transfers between devices  9.09 us (1%)
    reduce_scatter x1, waiting for transfers between devices, on_device(): lax.psum_scatter(expert_grad.astype(jnp.bfloat16), ('seq', 'mp'), scatter...  236 us
    all_gather x1, waiting for transfers between devices, on_device(): lax.all_gather(token_recv, ('seq', 'mp'), axis=0, tiled=True)  88.6 us
    unnamed x1, blocking collectives  57.6 us
    all_gather x1, waiting for transfers between devices, on_device(): lax.all_gather(grad_recv, ('seq', 'mp'), axis=0, tiled=True)  53.8 us
    all_gather x1, blocking collectives, on_device(): lax.all_gather(gate_recv, ('seq', 'mp'), axis=0, tiled=True)  30.7 us
    reshape x1, local copies, waits for them, and re-layouts, on_device(): token_all = token_all.reshape(-1, width)  23.6 us
    reshape x1, local copies, waits for them, and re-layouts, on_device(): grad_all = grad_all.reshape(-1, width)  23.5 us
    all_to_all x1, blocking collectives, on_device(): lax.all_to_all(dot_own.reshape(expert_count, capacity).astype(jnp.bfloat1...  23.4 us
  transfers between devices with their start and end apart: 4, of which 4 were waited for; matrix products, arithmetic and copies ran while one was open for 8% of the time, Pallas kernels for 0%

commit v1 on v0

--- a/solution.py
+++ b/solution.py
@@ -42,7 +42,12 @@
     token_all, grad_all, gate_all = (
         lax.all_gather(token_recv, ("seq", "mp"), axis=0, tiled=True),
         lax.all_gather(grad_recv, ("seq", "mp"), axis=0, tiled=True),
-        lax.all_gather(gate_recv, ("seq", "mp"), axis=0, tiled=True),
+        jnp.concatenate(
+            lax.all_to_all(
+                jnp.stack([gate_recv] * lax.axis_size(("seq", "mp"))), ("seq", "mp"), 0, 0
+            ),
+            axis=0,
+        ),
     )
     token_all = token_all.reshape(-1, width)
     grad_all = grad_all.reshape(-1, width)

time: 690 us -> 660 us (0.957)
  blocking collectives: 144 us -> 128 us
  waiting for transfers between devices: 384 us -> 370 us
    all_gather x1 -> x0, blocking collectives: 30.7 us -> none  [on_device(): lax.all_gather(gate_recv, ('seq', 'mp'), axis=0, tiled=True)]
    reduce_scatter x1, waiting for transfers between devices: 236 us -> 221 us  [on_device(): lax.psum_scatter(expert_grad.astype(jnp.bfloat16), ('seq', 'mp'), scatter...]
    all_to_all x0 -> x1, blocking collectives: none -> 14.2 us  [on_device(): lax.all_to_all(jnp.stack([gate_recv] * lax.axis_size(('seq', 'mp'))), ('s...]
where the time goes in v1:
time: 660 us; the launch traced here: 658 us
  waiting for transfers between devices  370 us (56%)
  blocking collectives  128 us (19%)
  local copies, waits for them, and re-layouts  85.1 us (13%)
  matrix products  48.3 us (7%)
  between operations  14.5 us (2%)
  starting transfers between devices  9.4 us (1%)
    reduce_scatter x1, waiting for transfers between devices, on_device(): lax.psum_scatter(expert_grad.astype(jnp.bfloat16), ('seq', 'mp'), scatter...  221 us
    all_gather x1, waiting for transfers between devices, on_device(): lax.all_gather(token_recv, ('seq', 'mp'), axis=0, tiled=True)  88.6 us
    unnamed x1, blocking collectives  57.6 us
    all_gather x1, waiting for transfers between devices, on_device(): lax.all_gather(grad_recv, ('seq', 'mp'), axis=0, tiled=True)  53.8 us
    reshape x1, local copies, waits for them, and re-layouts, on_device(): token_all = token_all.reshape(-1, width)  23.6 us
    reshape x1, local copies, waits for them, and re-layouts, on_device(): grad_all = grad_all.reshape(-1, width)  23.5 us
    all_to_all x1, blocking collectives, on_device(): lax.all_to_all(dot_own.reshape(expert_count, capacity).astype(jnp.bfloat1...  23.4 us
    all_gather x1, local copies, waits for them, and re-layouts, on_device(): lax.all_gather(token_recv, ('seq', 'mp'), axis=0, tiled=True)  14.7 us
  transfers between devices with their start and end apart: 4, of which 4 were waited for; matrix products, arithmetic and copies ran while one was open for 8% of the time, Pallas kernels for 0%

profile of v1, /device:TPU:1, one launch (start us, length us, event | category | flops | bytes accessed | tf_op | source)
XLA Modules:
  0.0 658.3 jit_solution(3475034274956067598)
XLA Ops:
  11.1 13.9 %all_to_all.38 = bf16[8,3,6144]{2,1,0:T(4,128)(2,1)S(1)} all-to-all(bf16[8,3,6144]{2,1,0:T(4,128)(2,1)S(1)} %copy.65), channel_id=1, replica_groups=mesh['seq'=8,'expert'=8,'mp'=4] {'expert'}, dimensions={0} | all-to-all | bytes 589824 | tf_op jit(solution)/shard_map/all_to_all | solution.py:38
  27.4 11.3 %all_to_all.39 = bf16[8,3,6144]{2,1,0:T(4,128)(2,1)S(1)} all-to-all(bf16[8,3,6144]{2,1,0:T(4,128)(2,1)S(1)} %copy.61), channel_id=1, replica_groups=mesh['seq'=8,'expert'=8,'mp'=4] {'expert'}, dimensions={0} | all-to-all | bytes 589824 | tf_op jit(solution)/shard_map/all_to_all | solution.py:39
  39.7 1.3 dynamic-slice
  41.7 88.6 %all-gather.5.cloned.1.call-done = bf16[256,3,6144]{2,0,1:T(8,128)(2,1)} async-done(((bf16[8,3,6144]{2,0,1:T(8,128)(2,1)}), bf16[256,3,6144]{2,0,1:T(8,128)(2,1)}) %all-gather.5.cloned.1.call-update) | async-done | bytes 9437200 | tf_op jit(solution)/shard_map/all_gather | solution.py:43
  130.3 14.7 %copy.67 = bf16[256,3,6144]{2,1,0:T(4,128)(2,1)} copy(bf16[256,3,6144]{2,0,1:T(8,128)(2,1)} %all-gather.5.cloned.1.call-done) | data formatting | bytes 18874368 | tf_op jit(solution)/shard_map/all_gather | solution.py:43
  145.0 23.6 %reshape.181 = bf16[768,6144]{1,0:T(8,128)(2,1)} reshape(bf16[256,3,6144]{2,1,0:T(4,128)(2,1)} %copy.67) | data formatting | bytes 18874368 | tf_op jit(solution)/shard_map/reshape | solution.py:52
  168.5 7.4 %fusion.4 = f32[768,256]{0,1:T(8,128)} fusion(bf16[768,6144]{1,0:T(8,128)(2,1)} %reshape.181, bf16[1,6144,256]{2,1,0:T(8,128)(2,1)S(1)} %copy-done), kind=kOutput, calls=%fused_computation.9 | convolution fusion | flops 2415919104 | bytes 13369344 | tf_op jit(solution)/shard_map/dot_general | solution.py:58
  175.9 3.8 fusion.7
  179.7 53.8 %all-gather.3.cloned.1.call-done = bf16[256,3,6144]{2,0,1:T(8,128)(2,1)} async-done(((bf16[8,3,6144]{2,0,1:T(8,128)(2,1)}), bf16[256,3,6144]{2,0,1:T(8,128)(2,1)}) %all-gather.3.cloned.1.call-update) | async-done | bytes 9437200 | tf_op jit(solution)/shard_map/all_gather | solution.py:44
  233.5 14.7 %copy.63 = bf16[256,3,6144]{2,1,0:T(4,128)(2,1)} copy(bf16[256,3,6144]{2,0,1:T(8,128)(2,1)} %all-gather.3.cloned.1.call-done) | data formatting | bytes 18874368 | tf_op jit(solution)/shard_map/all_gather | solution.py:44
  248.2 23.5 %reshape.180 = bf16[768,6144]{1,0:T(8,128)(2,1)} reshape(bf16[256,3,6144]{2,1,0:T(4,128)(2,1)} %copy.63) | data formatting | bytes 18874368 | tf_op jit(solution)/shard_map/reshape | solution.py:53
  271.7 8.6 %multiply_reduce_fusion = (f32[768]{0:T(1024)S(1)}, f32[768,256]{0,1:T(8,128)}) fusion(f32[768,256]{0,1:T(8,128)} %fusion.7, f32[768,256]{0,1:T(8,128)} %fusion.4, bf16[768,6144]{1,0:T(8,128)(2,1)} %reshape.180, bf16[1,256,6144]{2,1,0:T(8,128)(2,1)} %param.15), kind=kOutput, calls=%fused_computation.16 | convolution fusion | flops 2417294592 | bytes 14945280 | tf_op jit(solution)/shard_map/dot_general | solution.py:63
  280.3 57.6 %all-reduce = bf16[768]{0:T(1024)(128)(2,1)S(1)} all-reduce(f32[768]{0:T(1024)S(1)} %get-tuple-element.13), channel_id=3, replica_groups=mesh['seq'=8,'expert'=8,'mp'=4] {'seq','mp'}, use_global_device_ids=true, to_apply=%region_5.6.clone | all-reduce | flops 768 | bytes 4608
  338.0 23.4 %all_to_all.40 = bf16[8,1,3]{2,1,0:T(2,128)(2,1)S(1)} all-to-all(bf16[8,1,3]{2,1,0:T(2,128)(2,1)S(1)} %convert_element_type.107), channel_id=1, replica_groups=mesh['seq'=8,'expert'=8,'mp'=4] {'expert'}, dimensions={0} | all-to-all | bytes 96 | tf_op jit(solution)/shard_map/all_to_all | solution.py:82
  362.6 7.6 %all_to_all.41 = bf16[8,1,3]{2,1,0:T(2,128)(2,1)S(1)} all-to-all(bf16[8,1,3]{2,1,0:T(2,128)(2,1)S(1)} %copy.56), channel_id=1, replica_groups=mesh['seq'=8,'expert'=8,'mp'=4] {'expert'}, dimensions={0} | all-to-all | bytes 96 | tf_op jit(solution)/shard_map/all_to_all | solution.py:40
  370.3 14.2 %all_to_all.42 = bf16[32,8,3]{1,2,0:T(4,128)(2,1)S(1)} all-to-all(bf16[32,8,3]{1,2,0:T(4,128)(2,1)S(1)} %stack.7), channel_id=1, replica_groups=mesh['seq'=8,'expert'=8,'mp'=4] {'seq','mp'}, dimensions={0} | all-to-all | bytes 3072 | tf_op jit(solution)/shard_map/all_to_all | solution.py:46
  385.0 9.7 %fusion.2 = f32[768,6144]{1,0:T(8,128)} fusion(bf16[1,6144,256]{2,1,0:T(8,128)(2,1)S(1)} %copy-done, f32[768,256]{0,1:T(8,128)} %fusion.4, f32[768,256]{0,1:T(8,128)} %fusion.7, f32[768,256]{0,1:T(8,128)} %get-tuple-element.14, f32[768]{0:T(1024)S(1)} %reshape.182), kind=kOutput, calls=%fused_computation.7 | convolution fusion | flops 2418081792 | bytes 24382464 | tf_op jit(solution)/shard_map/dot_general | solution.py:68
  394.7 14.2 %add_convert_fusion = bf16[768,6144]{1,0:T(8,128)(2,1)} fusion(f32[768,6144]{1,0:T(8,128)} %fusion.2, bf16[1,6144,256]{2,1,0:T(8,128)(2,1)} %param.14, f32[768,256]{0,1:T(8,128)} %get-tuple-element.14, f32[768]{0:T(1024)S(1)} %reshape.182, f32[768,256]{0,1:T(8,128)} %fusion.4), kind=kOutput, calls=%fused_computation | convolution fusion | flops 2426732544 | bytes 33033216 | tf_op jit(solution)/shard_map/dot_general | solution.py:69
  409.0 221.4 %reduce-scatter.2.cloned.1.call-done = bf16[24,6144]{1,0:T(8,128)(2,1)} async-done(((bf16[768,6144]{1,0:T(8,128)(2,1)}), bf16[24,6144]{1,0:T(8,128)(2,1)}) %reduce-scatter.2.cloned.1.call-update) | async-done | bytes 294928 | tf_op jit(solution)/shard_map/reduce_scatter | solution.py:70
  630.3 1.9 convert_element_type.102
  632.2 9.3 %all-to-all-start.4 = ((bf16[8,3,6144]{2,1,0:T(4,128)(2,1)}), bf16[8,3,6144]{2,1,0:T(4,128)(2,1)S(1)}, u32[]{:S(2)}, u32[]{:S(2)}) async-start(bf16[8,3,6144]{2,1,0:T(4,128)(2,1)} %convert_element_type.102), calls=%async_computation.5 | async-start | bytes 786432 | tf_op jit(solution)/shard_map/all_to_all | solution.py:75
  642.7 1.2 pad_maximum_fusion
  643.9 5.7 all-to-all-done.4
  649.9 1.8 fusion.1
  (63 shorter events, 10.8 us)
Async XLA Ops:
  7.2 161.4 %copy-start = (bf16[1,6144,256]{2,1,0:T(8,128)(2,1)S(1)}, bf16[1,6144,256]{2,1,0:T(8,128)(2,1)}, u32[]{:S(2)}) copy-start(bf16[1,6144,256]{2,1,0:T(8,128)(2,1)} %param.13) | copy-start | bytes 9437188
  7.2 123.1 %all-gather.5.cloned.1.call-start = ((), (), s32[]{:S(2)}) async-start(), calls=%async_computation.8 | async-start | bytes 9732096 | tf_op jit(solution)/shard_map/all_gather | solution.py:43
  8.8 0.5 copy-start.5
  25.9 207.6 %all-gather.3.cloned.1.call-start = ((), (), s32[]{:S(2)}) async-start(), calls=%async_computation.7 | async-start | bytes 9732096 | tf_op jit(solution)/shard_map/all_gather | solution.py:44
  39.7 590.7 %reduce-scatter.2.cloned.1.call-start = ((), (), s32[]{:S(2)}) async-start(), calls=%async_computation.9 | async-start | bytes 9732096 | tf_op jit(solution)/shard_map/reduce_scatter | solution.py:70
  168.5 7.4 %copy-start.1 = (bf16[768,6144]{1,0:T(8,128)(2,1)S(1)}, bf16[768,6144]{1,0:T(8,128)(2,1)}, u32[]{:S(2)}) copy-start(bf16[768,6144]{1,0:T(8,128)(2,1)} %reshape.181) | copy-start | bytes 28311556
  168.5 7.4 %copy-start.2 = (bf16[1,6144,256]{2,1,0:T(8,128)(2,1)S(1)}, bf16[1,6144,256]{2,1,0:T(8,128)(2,1)}, u32[]{:S(2)}) copy-start(bf16[1,6144,256]{2,1,0:T(8,128)(2,1)} %param.14) | copy-start | bytes 9437188
  271.7 89.9 %copy-start.3 = (bf16[8,6144]{1,0:T(8,128)(2,1)S(1)}, bf16[8,6144]{1,0:T(8,128)(2,1)}, u32[]{:S(2)}) copy-start(bf16[8,6144]{1,0:T(8,128)(2,1)} %param.8) | copy-start | bytes 294916
  271.7 89.9 %copy-start.4 = (bf16[6144,8]{0,1:T(8,128)(2,1)S(1)}, bf16[6144,8]{0,1:T(8,128)(2,1)}, u32[]{:S(2)}) copy-start(bf16[6144,8]{0,1:T(8,128)(2,1)} %param.12) | copy-start | bytes 294916
  271.7 90.1 %copy-start.11 = (s32[8]{0:T(128)S(1)}, s32[8]{0:T(128)}, u32[]{:S(2)}) copy-start(s32[8]{0:T(128)} %param.10) | copy-start | bytes 100
  361.8 32.9 %copy-start.7 = (f32[8]{0:T(128)}, f32[8]{0:T(128)S(1)}, u32[]{:S(2)}) copy-start(f32[8]{0:T(128)S(1)} %get-tuple-element.6) | copy-start | bytes 100
  361.8 32.9 %copy-start.8 = (f32[8]{0:T(128)}, f32[8]{0:T(128)S(1)}, u32[]{:S(2)}) copy-start(f32[8]{0:T(128)S(1)} %get-tuple-element.7) | copy-start | bytes 100
  362.4 32.3 %copy-start.9 = (f32[8]{0:T(128)}, f32[8]{0:T(128)S(1)}, u32[]{:S(2)}) copy-start(f32[8]{0:T(128)S(1)} %get-tuple-element.9) | copy-start | bytes 100
  362.4 32.3 %copy-start.10 = (f32[8]{0:T(128)}, f32[8]{0:T(128)S(1)}, u32[]{:S(2)}) copy-start(f32[8]{0:T(128)S(1)} %get-tuple-element.10) | copy-start | bytes 100
  632.2 17.4 %all-to-all-start.4 = ((bf16[8,3,6144]{2,1,0:T(4,128)(2,1)}), bf16[8,3,6144]{2,1,0:T(4,128)(2,1)S(1)}, u32[]{:S(2)}, u32[]{:S(2)}) async-start(bf16[8,3,6144]{2,1,0:T(4,128)(2,1)} %convert_element_type.102), calls=%async_computation.5 | async-start | bytes 786432 | tf_op jit(solution)/shard_map/all_to_all | solution.py:75
  642.2 0.5 copy-start.6
Sparse Core Ops, SparseCore 0:
  26.0 104.1 all-gather.4
  132.9 100.5 all-gather.2
  409.1 221.2 reduce-scatter.1
